TPU v7x, 32 devices: a whole 2x2x4 slice. The times are simulated.
32 devices in a mesh: groups: 2 (over x), tensor: 4 (over y, core), dp: 4 (over z).
Axes of the slice: x: 2, y: 2, z: 4, core: 2. Of those that a mesh axis runs over, the one named last changes fastest.
Arguments:
- first_out: bfloat16 [4096, 1024], P(('groups', 'tensor', 'dp')), parts along dimension 0, may hold values from -6 to 6
- second_out: bfloat16 [4096, 1024], P(('groups', 'tensor', 'dp')), parts along dimension 0, may hold values from -6 to 6
- grad_first: bfloat16 [4096, 1024], P(('groups', 'tensor', 'dp')), parts along dimension 0, may hold values from -6 to 6
- grad_second: bfloat16 [4096, 1024], P(('groups', 'tensor', 'dp')), parts along dimension 0, may hold values from -6 to 6
- w_up: bfloat16 [1024, 8192], P('dp', 'tensor'), may hold values from -0.1875 to 0.1875
- w_down: bfloat16 [8192, 1024], P('tensor', 'dp'), may hold values from -0.0625 to 0.0625
- norm_gain: float32 [1024], replicated, may hold values from 0.25 to 1.75
- norm_bias: float32 [1024], replicated, may hold values from -3 to 3
Outputs:
- second_in: bfloat16 [4096, 1024], P(('groups', 'tensor', 'dp')), parts along dimension 0
- grad_first_in: float32 [4096, 1024], P(('groups', 'tensor', 'dp')), parts along dimension 0
- grad_up: float32 [2048, 8192], P(('groups', 'dp'), 'tensor'), parts along dimension 0
- grad_down: float32 [16384, 1024], P(('groups', 'tensor'), 'dp'), parts along dimension 0
- grad_norm: float32 [4, 1024], P('groups'), parts along dimension 0
There are 2 independent parts, one for each index of `groups`. A program takes and returns all parts, laid end to end along the dimension named above; an argument that names none is the same for every part. Nothing has to cross between parts.
All inputs are finite; a program needn't handle non-finite values.
Results may differ from a plain program's by a relative error of at most 0.017.
Values may be sent and summed in bfloat16 or wider, within the bound.
A program may use at most 64 MiB of HBM per device.

v0:
```python
import functools

import jax
import jax.numpy as jnp
import numpy as np
from jax import lax
from jax.experimental import pallas as pl
from jax.experimental.pallas import tpu as pltpu
from jax.sharding import PartitionSpec as P

epsilon = 1e-06


def normalize(row_data, norm_gain, norm_bias):
    values = row_data.astype(jnp.float32)
    row_mean = jnp.mean(values, axis=-1, keepdims=True)
    centred = values - row_mean
    inv_std = lax.rsqrt(jnp.mean(centred * centred, axis=-1, keepdims=True) + epsilon)
    standard = centred * inv_std
    normed = (standard * norm_gain + norm_bias).astype(jnp.bfloat16)
    return (standard, inv_std, normed)


def contract_tokens(left_rows, right_rows):
    return lax.dot_general(
        left_rows, right_rows, (((0,), (0,)), ((), ())), preferred_element_type=jnp.float32
    )


def body(first_out, second_out, grad_first, grad_second, w_up, w_down, norm_gain, norm_bias):
    own_rows = first_out.shape[0]
    up_full, down_full = (
        lax.all_gather(w_up, "dp", axis=0, tiled=True),
        lax.all_gather(w_down, "dp", axis=1, tiled=True),
    )
    first_all, grad_all = (
        lax.all_gather(first_out, "tensor", axis=0, tiled=True),
        lax.all_gather(grad_second, "tensor", axis=0, tiled=True),
    )
    standard_all, inv_std_all, normed = normalize(first_all, norm_gain, norm_bias)
    offset = lax.axis_index("tensor") * own_rows
    standard = lax.dynamic_slice_in_dim(standard_all, offset, own_rows, 0)
    inv_std = lax.dynamic_slice_in_dim(inv_std_all, offset, own_rows, 0)
    preact = jnp.dot(normed, up_full, preferred_element_type=jnp.float32)
    hidden = jax.nn.gelu(preact).astype(jnp.bfloat16)
    branch = lax.psum_scatter(
        jnp.dot(hidden, down_full, preferred_element_type=jnp.float32).astype(jnp.bfloat16),
        "tensor",
        scatter_dimension=0,
        tiled=True,
    ).astype(jnp.float32)
    second_in = (second_out.astype(jnp.float32) - branch).astype(jnp.bfloat16)
    tokens = own_rows * lax.axis_size("tensor") * lax.axis_size("dp")
    grad_scale = tokens ** (-0.5)
    grad_down_part = contract_tokens(hidden, grad_all)
    grad_down = (
        lax.psum_scatter(
            grad_down_part.astype(jnp.bfloat16), "dp", scatter_dimension=1, tiled=True
        ).astype(jnp.float32)
        * grad_scale
    )
    grad_hidden = lax.dot_general(
        grad_all, down_full, (((1,), (1,)), ((), ())), preferred_element_type=jnp.float32
    )
    grad_pre = jax.vjp(jax.nn.gelu, preact)[1](grad_hidden)[0].astype(jnp.bfloat16)
    grad_up_part = contract_tokens(normed, grad_pre)
    grad_up = (
        lax.psum_scatter(
            grad_up_part.astype(jnp.bfloat16), "dp", scatter_dimension=0, tiled=True
        ).astype(jnp.float32)
        * grad_scale
    )
    grad_normed = lax.psum_scatter(
        lax.dot_general(
            grad_pre, up_full, (((1,), (1,)), ((), ())), preferred_element_type=jnp.float32
        ).astype(jnp.bfloat16),
        "tensor",
        scatter_dimension=0,
        tiled=True,
    ).astype(jnp.float32)
    grad_std = grad_normed * norm_gain
    grad_rows = inv_std * (
        grad_std
        - jnp.mean(grad_std, axis=-1, keepdims=True)
        - standard * jnp.mean(grad_std * standard, axis=-1, keepdims=True)
    )
    grad_first_in = grad_first.astype(jnp.float32) + grad_rows
    local_stats = jnp.stack([jnp.sum(grad_normed * standard, axis=0), jnp.sum(grad_normed, axis=0)])
    grad_norm = lax.psum(local_stats, ("tensor", "dp")) * grad_scale
    return (second_in, grad_first_in, grad_up, grad_down, grad_norm)


def span(index, size):
    return pl.ds(pl.multiple_of(index * size, size), size)


def flipped(index, mask, bits):
    for bit in range(bits):
        if mask >> bit & 1:
            step = 1 << bit
            index = index + (1 - 2 * ((index // step) % 2)) * step
    return index


def greet(n_groups, n_dp, bits, group, tensor, dp):
    barrier = pltpu.get_barrier_semaphore()
    peers = [{"dp": (dp + s) % n_dp} for s in range(1, n_dp)]
    peers += [{"tensor": flipped(tensor, 1 << bit, bits)} for bit in range(bits)]
    peers += [{"groups": (group + s) % n_groups} for s in range(1, n_groups)]
    for peer in peers:
        pl.semaphore_signal(
            barrier, inc=1, device_id=peer, device_id_type=pl.DeviceIdType.MESH
        )
    pl.semaphore_wait(barrier, len(peers))


def remote(src, dst, sems, index, peer):
    return pltpu.make_async_remote_copy(
        src_ref=src,
        dst_ref=dst,
        send_sem=sems[0].at[index],
        recv_sem=sems[1].at[index],
        device_id=peer,
        device_id_type=pl.DeviceIdType.MESH,
    )


def gather_tokens(
    n_groups, n_tensor, n_dp, use,
    first_ref, grad_ref, w_up_ref, w_down_ref, gain_ref, bias_ref,
    normed_all, grad_all, up_ref, down_ref,
    own_normed, local_sem, line_send, line_recv, column_send, column_recv,
    weight_send, weight_recv, share_send, share_recv,
):
    group, tensor, dp = (lax.axis_index(name) for name in ("groups", "tensor", "dp"))
    bits = n_tensor.bit_length() - 1
    rows = first_ref.shape[0]
    depth = w_up_ref.shape[0]
    units = w_up_ref.shape[1] // n_dp
    outputs = (normed_all, grad_all)
    line_sems, column_sems = (line_send, line_recv), (column_send, column_recv)
    weight_sems, share_sems = (weight_send, weight_recv), (share_send, share_recv)

    def block(a, mask, source):
        return outputs[a].at[span(flipped(tensor, mask, bits) * n_dp + source, rows), :]

    def place(k):
        if k == 0:
            return dp, None
        if k < n_dp:
            return dp - k, dp >= k
        return dp + (k - n_dp + 1), dp + (k - n_dp + 1) <= n_dp - 1

    def guarded(conditions, action):
        conditions = [c for c in conditions if c is not None]
        if not conditions:
            action()
        else:
            pl.when(functools.reduce(jnp.logical_and, conditions))(action)

    def line_copy(a, side, distance):
        if side == 0:
            source, target = dp - (distance - 1), dp + 1
        else:
            source, target = dp + (distance - 1), dp - 1
        src = grad_ref if a == 1 and distance == 1 else block(a, 0, source)
        return remote(src, block(a, 0, source), line_sems, (a, side, distance), {"dp": target})

    def line_send_conditions(side, distance):
        if side == 0:
            return [dp >= distance - 1 if distance > 1 else None, dp <= n_dp - 2]
        return [dp <= n_dp - distance if distance > 1 else None, dp >= 1]

    def column_copy(a, mask, k, bit):
        source, _ = place(k)
        src = grad_ref if a == 1 and mask == 0 and k == 0 else block(a, mask, source)
        return remote(
            src, block(a, mask, source), column_sems, (a, mask | 1 << bit, k),
            {"tensor": flipped(tensor, 1 << bit, bits)},
        )

    def column_arrival(a, mask, k):
        source, _ = place(k)
        bit = (mask & -mask).bit_length() - 1
        here = block(a, mask, source)
        return remote(
            here, here, column_sems, (a, mask, k), {"tensor": flipped(tensor, 1 << bit, bits)}
        )

    def next_bits(mask):
        top = bits if mask == 0 else (mask & -mask).bit_length() - 1
        return list(reversed(range(top)))

    def pass_on(a, mask, k):
        for bit in next_bits(mask):
            column_copy(a, mask, k, bit).start()

    part = depth // n_groups
    piece = units // n_groups

    def weight_views(kind, source, owner):
        if kind == 0:
            return up_ref.at[span(source * n_groups + owner, part), :]
        return down_ref.at[span(owner, piece), span(source, depth)]

    def weight_copy(kind, s):
        target = (dp + s) % n_dp
        if kind == 0:
            src = w_up_ref.at[span(group, part), span(target, units)]
        else:
            src = w_down_ref.at[span(target * n_groups + group, piece), :]
        return remote(src, weight_views(kind, dp, group), weight_sems, (kind, s), {"dp": target})

    def weight_arrival(kind, s):
        here = weight_views(kind, (dp + n_dp - s) % n_dp, group)
        return remote(here, here, weight_sems, (kind, s), {"dp": (dp + s) % n_dp})

    def share_copy(kind, s, h):
        here = weight_views(kind, (dp + n_dp - s) % n_dp, group)
        return remote(here, here, share_sems, (kind, s, h), {"groups": (group + h) % n_groups})

    def share_arrival(kind, s, h):
        here = weight_views(kind, (dp + n_dp - s) % n_dp, (group + n_groups - h) % n_groups)
        return remote(here, here, share_sems, (kind, s, h), {"groups": (group + h) % n_groups})

    greet(n_groups, n_dp, bits, group, tensor, dp)
    order = [0] + [k for s in range(1, n_dp) for k in (s, s + n_dp - 1)]
    def send_own(a):
        for side in range(2):
            guarded(
                line_send_conditions(side, 1), lambda side=side: line_copy(a, side, 1).start()
            )
        pass_on(a, 0, 0)

    send_own(1)
    local = [
        pltpu.make_async_copy(grad_ref, block(1, 0, dp), local_sem.at[1]),
        pltpu.make_async_copy(
            w_up_ref.at[:, span(dp, units)], up_ref.at[span(dp, depth), :], local_sem.at[2]
        ),
        pltpu.make_async_copy(
            w_down_ref.at[span(dp, units), :], down_ref.at[:, span(dp, depth)], local_sem.at[3]
        ),
    ]
    for copy in local:
        copy.start()

    @pl.loop(0, rows // 16)
    def _(i):
        cut = pl.ds(pl.multiple_of(i * 16, 16), 16)
        standard, _ = standardize(first_ref[cut, :])
        own_normed[cut, :] = (standard * gain_ref[...] + bias_ref[...]).astype(own_normed.dtype)

    settle = pltpu.make_async_copy(own_normed, block(0, 0, dp), local_sem.at[0])
    settle.start()
    settle.wait()
    send_own(0)
    for s in range(1, n_dp):
        for kind in range(2):
            weight_copy(kind, s).start()

    through = [m for m in range(1, n_tensor) if next_bits(m)]
    final = [m for m in range(1, n_tensor) if not next_bits(m)]

    def relay(k):
        for a in range(2):
            for mask in sorted(through, reverse=True):
                def action(a=a, mask=mask):
                    column_arrival(a, mask, k).wait_recv()
                    pass_on(a, mask, k)
                guarded([place(k)[1]], action)

    done = [[0]] + [[s, s + n_dp - 1] for s in range(1, n_dp)]
    for s in range(1, n_dp):
        for a in range(2):
            for side in range(2):
                k = done[s][side]

                def action(a=a, side=side, k=k, s=s):
                    source, _ = place(k)
                    here = block(a, 0, source)
                    remote(here, here, line_sems, (a, side, s), {"dp": (dp + 1) % n_dp}).wait_recv()
                    if s < n_dp - 1:
                        guarded(
                            line_send_conditions(side, s + 1),
                            lambda: line_copy(a, side, s + 1).start(),
                        )
                    pass_on(a, 0, k)

                guarded([place(k)[1]], action)
        for k in done[s - 1]:
            relay(k)
        for kind in range(2):
            weight_arrival(kind, s).wait_recv()
            for h in range(1, n_groups):
                share_copy(kind, s, h).start()
    for k in done[n_dp - 1]:
        relay(k)
    for copy in local:
        copy.wait()
    for s in range(1, n_dp):
        for kind in range(2):
            for h in range(1, n_groups):
                share_arrival(kind, s, h).wait_recv()
    for mask in [0] + through:
        use(mask)
    for mask in final:
        for k in order:
            for a in range(2):
                guarded(
                    [place(k)[1]], lambda a=a, mask=mask, k=k: column_arrival(a, mask, k).wait_recv()
                )
        use(mask)
    for s in range(1, n_dp):
        for kind in range(2):
            weight_copy(kind, s).wait_send()
            for h in range(1, n_groups):
                share_copy(kind, s, h).wait_send()
    for a in range(2):
        for side in range(2):
            for s in range(1, n_dp):
                guarded(
                    line_send_conditions(side, s),
                    lambda a=a, side=side, s=s: line_copy(a, side, s).wait_send(),
                )
        for mask in [0] + through:
            for k in order:
                for bit in next_bits(mask):
                    guarded(
                        [place(k)[1]],
                        lambda a=a, mask=mask, k=k, bit=bit: column_copy(a, mask, k, bit).wait_send(),
                    )


def scatter_sums(
    n_groups, n_tensor, n_dp, grad_scale, weight_block,
    hidden_ref, pre_ref, up_ref, down_ref, g_up_ref, g_down_ref,
    first_ref, second_ref, grad_ref, gain_ref,
    second_in_ref, grad_first_ref, grad_norm_ref, up_out, down_out,
    partials, fold, right, left, stat_line, stat_fold, local_sem,
    fold_send, fold_recv, line_send, line_recv, grads_send, grads_recv,
    stat_send, stat_recv, pair_send, pair_recv,
):
    group, tensor, dp = (lax.axis_index(name) for name in ("groups", "tensor", "dp"))
    bits = n_tensor.bit_length() - 1
    rows, width = first_ref.shape
    units = g_up_ref.shape[2]
    depth = g_up_ref.shape[1]
    fold_sems, line_sems = (fold_send, fold_recv), (line_send, line_recv)
    grads_sems, stat_sems, pair_sems = (
        (grads_send, grads_recv), (stat_send, stat_recv), (pair_send, pair_recv),
    )
    slots = {}
    for bit in range(bits):
        for mask in range(0, n_tensor, 2 << bit):
            slots[bit, mask] = len(slots)

    def grads_copy(kind, s):
        target = (dp + s) % n_dp
        if kind == 0:
            src, dst = g_up_ref.at[target], up_out.at[:, span(dp, units)]
        else:
            src, dst = g_down_ref.at[target], down_out.at[span(dp, units), :]
        return remote(src, dst, grads_sems, (kind, s), {"dp": target})

    def grads_arrival(kind, s):
        source = (dp + n_dp - s) % n_dp
        here = up_out.at[:, span(source, units)] if kind == 0 else down_out.at[span(source, units), :]
        return remote(here, here, grads_sems, (kind, s), {"dp": (dp + s) % n_dp})

    def current(a, bit, mask, b):
        if bit == 0:
            return partials.at[a, mask, b]
        return fold.at[a, slots[bit - 1, mask], b]

    def fold_copy(a, bit, mask, b):
        slot = slots[bit, mask ^ 1 << bit]
        return remote(
            current(a, bit, mask, b), fold.at[a, slot, b], fold_sems, (a, slot, b),
            {"tensor": flipped(tensor, 1 << bit, bits)},
        )

    def fold_arrival(a, bit, mask, b):
        slot = slots[bit, mask]
        here = fold.at[a, slot, b]
        return remote(
            here, here, fold_sems, (a, slot, b), {"tensor": flipped(tensor, 1 << bit, bits)}
        )

    def add_into(ref, other):
        @pl.loop(0, rows // 16)
        def _(i):
            cut = pl.ds(pl.multiple_of(i * 16, 16), 16)
            ref[cut, :] = (
                ref[cut, :].astype(jnp.float32) + other[cut, :].astype(jnp.float32)
            ).astype(ref.dtype)

    def sent_masks(bit):
        masks = [m for m in range(n_tensor) if m % (1 << bit) == 0 and m >> bit & 1]
        return sorted(masks, reverse=True)

    def kept_masks(bit):
        return sorted(range(0, n_tensor, 2 << bit), reverse=True)

    @pl.loop(1, n_dp)
    def _(s):
        weight_block(0, (dp + s) % n_dp)
        grads_copy(0, s).start()

    way = 2 * ((2 * dp) // n_dp) - 1

    def multiply(mask, b):
        cut = span(flipped(tensor, mask, bits) * n_dp + b, rows)
        partials[0, mask, b] = jnp.dot(
            hidden_ref[cut, :], down_ref[...], preferred_element_type=jnp.float32
        ).astype(partials.dtype)
        partials[1, mask, b] = lax.dot_general(
            pre_ref[cut, :], up_ref[...], (((1,), (1,)), ((), ())),
            preferred_element_type=jnp.float32,
        ).astype(partials.dtype)

    def folded(bit, mask, b):
        for a in range(2):
            fold_arrival(a, bit, mask, b).wait_recv()
            add_into(fold.at[a, slots[bit, mask], b], current(a, bit, mask, b))
            if bit + 1 < bits and mask in sent_masks(bit + 1):
                fold_copy(a, bit + 1, mask, b).start()

    for mask in sent_masks(0):
        @pl.loop(0, n_dp)
        def _(i, mask=mask):
            b = (dp + way * (1 + i) + n_dp) % n_dp
            multiply(mask, b)
            for a in range(2):
                fold_copy(a, 0, mask, b).start()

        @pl.loop(0, n_dp)
        def _(i, mask=mask):
            b = (dp + way * (1 + i) + n_dp) % n_dp
            multiply(mask - 1, b)
            folded(0, mask - 1, b)

    for bit in range(1, bits - 1):
        for mask in kept_masks(bit):
            for i in range(n_dp):
                folded(bit, mask, (dp + way * (1 + i) + n_dp) % n_dp)

    def finish(b):
        if bits > 1:
            folded(bits - 1, 0, b)

    last = slots[bits - 1, 0]
    moving = (right, left)

    def line_conditions(side, s):
        return dp + s <= n_dp - 1 if side == 0 else dp >= s

    def behind(side):
        return dp >= 1 if side == 0 else dp <= n_dp - 2

    def line_peer(side):
        return {"dp": (dp + 1) % n_dp if side == 0 else (dp + n_dp - 1) % n_dp}

    def line_copy(a, side, s, relayed):
        target = dp + s if side == 0 else dp - s
        src = moving[side].at[a, s] if relayed else fold.at[a, last, target]
        return remote(src, moving[side].at[a, s - 1], line_sems, (a, side, s - 1), line_peer(side))

    def line_arrival(a, side, s):
        here = moving[side].at[a, s]
        return remote(here, here, line_sems, (a, side, s), line_peer(side))

    for s in range(n_dp - 1, 0, -1):
        weight_block(1, (dp + s) % n_dp)
        for side in range(2):
            @pl.when(jnp.logical_and(line_conditions(side, s), jnp.logical_not(behind(side))))
            def _(side=side, s=s):
                finish(dp + s if side == 0 else dp - s)
                for a in range(2):
                    line_copy(a, side, s, False).start()

            if s <= n_dp - 2:
                @pl.when(jnp.logical_and(line_conditions(side, s), behind(side)))
                def _(side=side, s=s):
                    target = dp + s if side == 0 else dp - s
                    finish(target)
                    for a in range(2):
                        line_arrival(a, side, s).wait_recv()
                        add_into(moving[side].at[a, s], fold.at[a, last, target])
                        line_copy(a, side, s, True).start()
        grads_copy(1, s).start()
    weight_block(0, dp)
    weight_block(1, dp)
    local = [
        pltpu.make_async_copy(g_up_ref.at[dp], up_out.at[:, span(dp, units)], local_sem.at[0]),
        pltpu.make_async_copy(g_down_ref.at[dp], down_out.at[span(dp, units), :], local_sem.at[1]),
    ]
    for copy in local:
        copy.start()
    finish(dp)

    for a in range(2):
        for side in range(2):
            @pl.when(behind(side))
            def _(a=a, side=side):
                line_arrival(a, side, 0).wait_recv()

            @pl.when(jnp.logical_not(behind(side)))
            def _(a=a, side=side):
                moving[side][a, 0] = jnp.zeros((rows, width), moving[side].dtype)

    stat_line[dp] = jnp.zeros(stat_line.shape[1:], jnp.float32)

    @pl.loop(0, rows // 16)
    def _(i):
        cut = pl.ds(pl.multiple_of(i * 16, 16), 16)

        def total(a):
            return (
                fold[a, last, dp, cut, :].astype(jnp.float32)
                + right[a, 0, cut, :].astype(jnp.float32)
                + left[a, 0, cut, :].astype(jnp.float32)
            )

        second_in_ref[cut, :] = (second_ref[cut, :].astype(jnp.float32) - total(0)).astype(
            second_in_ref.dtype
        )
        standard, inv_std = standardize(first_ref[cut, :])
        grad_normed = total(1)
        stat_line[dp, 0:1, :] += jnp.sum(grad_normed * standard, axis=0, keepdims=True)
        stat_line[dp, 1:2, :] += jnp.sum(grad_normed, axis=0, keepdims=True)
        grad_std = grad_normed * gain_ref[...]
        grad_rows = inv_std * (
            grad_std
            - jnp.mean(grad_std, axis=-1, keepdims=True)
            - standard * jnp.mean(grad_std * standard, axis=-1, keepdims=True)
        )
        grad_first_ref[cut, :] = grad_ref[cut, :].astype(jnp.float32) + grad_rows

    def stat_copy(s):
        here = stat_line.at[dp]
        return remote(here, here, stat_sems, s, {"dp": (dp + s) % n_dp})

    def stat_arrival(s):
        here = stat_line.at[(dp + n_dp - s) % n_dp]
        return remote(here, here, stat_sems, s, {"dp": (dp + s) % n_dp})

    for s in range(1, n_dp):
        stat_copy(s).start()
    for s in range(1, n_dp):
        stat_arrival(s).wait_recv()
    sums = stat_line[0]
    for source in range(1, n_dp):
        sums = sums + stat_line[source]
    for bit in range(bits):
        stat_fold[bit, 0] = sums
        copy = remote(
            stat_fold.at[bit, 0], stat_fold.at[bit, 1], pair_sems, bit,
            {"tensor": flipped(tensor, 1 << bit, bits)},
        )
        copy.start()
        copy.wait()
        sums = stat_fold[bit, 0] + stat_fold[bit, 1]
    grad_norm_ref[...] = sums[0:2] * grad_scale

    for s in range(1, n_dp):
        stat_copy(s).wait_send()
        for kind in range(2):
            grads_arrival(kind, s).wait_recv()
            grads_copy(kind, s).wait_send()
    for copy in local:
        copy.wait()
    for bit in range(bits):
        for mask in sent_masks(bit):
            for b in range(n_dp):
                for a in range(2):
                    fold_copy(a, bit, mask, b).wait_send()
    for s in range(n_dp - 1, 0, -1):
        for a in range(2):
            for side in range(2):
                @pl.when(line_conditions(side, s))
                def _(a=a, side=side, s=s):
                    line_copy(a, side, s, s <= n_dp - 2).wait_send()


def standardize(row_data):
    values = row_data.astype(jnp.float32)
    centred = values - jnp.mean(values, axis=-1, keepdims=True)
    inv_std = lax.rsqrt(jnp.mean(centred * centred, axis=-1, keepdims=True) + epsilon)
    return centred * inv_std, inv_std


def fused_kernel(
    n_groups, n_tensor, n_dp, grad_scale,
    first_ref, second_ref, grad_first_in_ref, grad_ref, w_up_ref, w_down_ref, gain_ref, bias_ref,
    second_in_ref, grad_first_ref, grad_norm_ref, up_out, down_out,
    normed_all, grad_all, up_ref, down_ref, hidden_ref, pre_ref, g_up_ref, g_down_ref,
    *scratch,
):
    tensor = lax.axis_index("tensor")
    bits = n_tensor.bit_length() - 1
    column = first_ref.shape[0] * n_dp
    chunk = column // 2
    depth = g_up_ref.shape[1]
    gather_count = 10

    def use(mask):
        base = flipped(tensor, mask, bits)

        @pl.loop(0, column // chunk)
        def _(i):
            cut = span(base * (column // chunk) + i, chunk)
            preact = jnp.dot(
                normed_all[cut, :], up_ref[...], preferred_element_type=jnp.float32
            )
            grad_hidden = lax.dot_general(
                grad_all[cut, :], down_ref[...], (((1,), (1,)), ((), ())),
                preferred_element_type=jnp.float32,
            )
            root = (2.0 / np.pi) ** 0.5
            square = preact * preact
            bend = jnp.tanh(root * (preact + 0.044715 * (square * preact)))
            gate = 0.5 * (1.0 + bend)
            hidden_ref[cut, :] = (preact * gate).astype(hidden_ref.dtype)
            slope = gate + (0.5 * preact) * (1.0 - bend * bend) * (
                root * (1.0 + 3.0 * 0.044715 * square)
            )
            pre_ref[cut, :] = (grad_hidden * slope).astype(pre_ref.dtype)

    def weight_block(kind, target):
        cut = span(target, depth)
        if kind == 0:
            g_up_ref[target] = contract_tokens(normed_all[:, cut], pre_ref[...]).astype(g_up_ref.dtype)
        else:
            g_down_ref[target] = contract_tokens(hidden_ref[...], grad_all[:, cut]).astype(
                g_down_ref.dtype
            )

    gather_tokens(
        n_groups, n_tensor, n_dp, use,
        first_ref, grad_ref, w_up_ref, w_down_ref, gain_ref, bias_ref,
        normed_all, grad_all, up_ref, down_ref, *scratch[:gather_count],
    )
    scatter_sums(
        n_groups, n_tensor, n_dp, grad_scale, weight_block,
        hidden_ref, pre_ref, up_ref, down_ref, g_up_ref, g_down_ref,
        first_ref, second_ref, grad_first_in_ref, gain_ref,
        second_in_ref, grad_first_ref, grad_norm_ref, up_out, down_out, *scratch[gather_count:],
    )


ANY = pl.BlockSpec(memory_space=pl.ANY)
VMEM = pl.BlockSpec(memory_space=pltpu.VMEM)
DMA = pltpu.SemaphoreType.DMA


def spread_body(sizes, first_out, second_out, grad_first, grad_second, w_up, w_down, norm_gain, norm_bias):
    n_groups, n_tensor, n_dp = sizes
    rows, width = first_out.shape
    tokens = rows * n_tensor * n_dp
    units = w_up.shape[1] // n_dp
    bits = n_tensor.bit_length() - 1
    half = jnp.bfloat16
    grad_scale = tokens ** (-0.5)
    gain, bias = norm_gain.reshape(1, -1), norm_bias.reshape(1, -1)
    depth = w_up.shape[0]
    second_in, grad_first_in, grad_norm, up_out, down_out = pl.pallas_call(
        functools.partial(fused_kernel, n_groups, n_tensor, n_dp, grad_scale),
        out_shape=(
            jax.ShapeDtypeStruct((rows, width), half),
            jax.ShapeDtypeStruct((rows, width), jnp.float32),
            jax.ShapeDtypeStruct((2, width), jnp.float32),
            jax.ShapeDtypeStruct(w_up.shape, half),
            jax.ShapeDtypeStruct(w_down.shape, half),
        ),
        in_specs=[VMEM] * 8,
        out_specs=(VMEM,) * 3 + (ANY,) * 2,
        scratch_shapes=[
            pltpu.VMEM((tokens, width), half),
            pltpu.VMEM((tokens, width), half),
            pltpu.VMEM((width, units), half),
            pltpu.VMEM((units, width), half),
            pltpu.VMEM((tokens, units), half),
            pltpu.VMEM((tokens, units), half),
            pltpu.VMEM((n_dp, depth, units), half),
            pltpu.VMEM((n_dp, units, depth), half),
        ]
        + [pltpu.VMEM((rows, width), half), DMA((4,))]
        + [DMA((2, 2, n_dp))] * 2
        + [DMA((2, n_tensor, 2 * n_dp - 1))] * 2
        + [DMA((2, n_dp))] * 2
        + [DMA((2, n_dp, n_groups))] * 2
        + [
            pltpu.VMEM((2, n_tensor, n_dp, rows, width), half),
            pltpu.VMEM((2, n_tensor - 1, n_dp, rows, width), half),
            pltpu.VMEM((2, n_dp - 1, rows, width), half),
            pltpu.VMEM((2, n_dp - 1, rows, width), half),
            pltpu.VMEM((n_dp, 8, width), jnp.float32),
            pltpu.VMEM((bits, 2, 8, width), jnp.float32),
            DMA((2,)),
        ]
        + [DMA((2, n_tensor - 1, n_dp))] * 2
        + [DMA((2, 2, n_dp - 1))] * 2
        + [DMA((2, n_dp))] * 2
        + [DMA((n_dp,))] * 2
        + [DMA((bits,))] * 2,
        compiler_params=pltpu.CompilerParams(
            collective_id=0, has_side_effects=True, vmem_limit_bytes=60 << 20
        ),
        name="spread_backward",
    )(first_out, second_out, grad_first, grad_second, w_up, w_down, gain, bias)
    grad_up = up_out.astype(jnp.float32) * grad_scale
    grad_down = down_out.astype(jnp.float32) * grad_scale
    return second_in, grad_first_in, grad_up, grad_down, grad_norm


def choose(sizes, *args):
    first_out, w_up = args[0], args[4]
    n_groups, n_tensor, n_dp = sizes
    tokens = first_out.shape[0] * n_tensor * n_dp
    fits = (
        n_tensor > 1
        and n_dp > 1
        and n_dp % 2 == 0
        and n_tensor & (n_tensor - 1) == 0
        and w_up.shape[1] % (n_dp * n_groups * 128) == 0
        and w_up.shape[0] % (n_groups * 128) == 0
    )
    if fits and tokens <= w_up.shape[1]:
        return spread_body(sizes, *args)
    return body(*args)


def solution(mesh):
    in_specs = (
        P(("groups", "tensor", "dp"), None),
        P(("groups", "tensor", "dp"), None),
        P(("groups", "tensor", "dp"), None),
        P(("groups", "tensor", "dp"), None),
        P("dp", "tensor"),
        P("tensor", "dp"),
        P(),
        P(),
    )
    out_specs = (
        P(("groups", "tensor", "dp"), None),
        P(("groups", "tensor", "dp"), None),
        P(("groups", "dp"), "tensor"),
        P(("groups", "tensor"), "dp"),
        P("groups", None),
    )
    sizes = tuple(mesh.shape[name] for name in ("groups", "tensor", "dp"))
    return jax.shard_map(functools.partial(choose, sizes), mesh=mesh, in_specs=in_specs, out_specs=out_specs, check_vma=False)
```

profile of v0, /device:TPU:0, one launch (start us, length us, event | category | flops | bytes accessed | tf_op | source)
XLA Modules:
  0.0 164.0 jit_solution(12689409481628773706)
XLA Ops:
  0.6 156.8 %spread_backward.1 = (bf16[128,1024]{1,0:T(8,128)(2,1)}, f32[128,1024]{1,0:T(8,128)}, f32[2,1024]{1,0:T(2,128)}, bf16[256,2048]{1,0:T(8,128)(2,1)}, bf16[2048,256]{1,0:T(8,128)(2,1)}) custom-call(bf16[128,1024]{1,0:T(8,128)(2,1)} %first_ref.1, bf16[128,1024]{1,0:T(8,128)(2,1)} %second_ref.1, bf16[128,1024]{1,0:T(8,128)(2,1)} %grad_first_in_ref.1, ...), custom_call_target="tpu_custom_call" | custom-call | tf_op jit(solution)/shard_map/spread_backward/pallas_call | solution.py:667
  157.5 0.0 copy-start
  157.5 2.9 %convert_multiply_fusion.1 = f32[256,2048]{1,0:T(8,128)} fusion(bf16[256,2048]{1,0:T(8,128)(2,1)} %get-tuple-element.12), kind=kLoop, calls=%fused_computation.1 | loop fusion | flops 1048576 | bytes 3145728 | tf_op jit(solution)/shard_map/mul | solution.py:712
  160.4 0.0 copy-done
  160.4 0.0 copy-start.2
  160.4 0.0 copy-start.1
  160.4 0.0 copy-start.3
  160.4 1.5 convert_multiply_fusion
  161.9 0.0 copy-done.2
  161.9 0.7 copy.16
  162.6 0.0 copy-done.1
  162.6 0.8 copy.17
  163.4 0.0 copy-done.3
  163.4 0.6 copy.18
Async XLA Ops:
  157.5 2.9 %copy-start = (bf16[2048,256]{1,0:T(8,128)(2,1)S(1)}, bf16[2048,256]{1,0:T(8,128)(2,1)}, u32[]{:S(2)}) copy-start(bf16[2048,256]{1,0:T(8,128)(2,1)} %get-tuple-element.13) | copy-start | bytes 3145732
  160.4 1.5 copy-start.2
  160.4 2.2 %copy-start.1 = (f32[128,1024]{1,0:T(8,128)S(1)}, f32[128,1024]{1,0:T(8,128)}, u32[]{:S(2)}) copy-start(f32[128,1024]{1,0:T(8,128)} %get-tuple-element.21) | copy-start | bytes 1572868
  160.4 3.0 %copy-start.3 = (f32[2,1024]{1,0:T(2,128)S(1)}, f32[2,1024]{1,0:T(2,128)}, u32[]{:S(2)}) copy-start(f32[2,1024]{1,0:T(2,128)} %get-tuple-element.24) | copy-start | bytes 24580
where the time goes:
time: 164 us
  Pallas kernels  157 us (96%)
  other arithmetic  4.39 us (3%)
  local copies, waits for them, and re-layouts  2.11 us (1%)
    pallas_call x1, Pallas kernels, spread_body(): pl.pallas_call(functools.partial(fused_kernel, n_groups, n_tensor, n_dp,...  157 us

commit v1 on v0

v1 whole, which is shorter than its diff:
```python
import functools

import jax
import jax.numpy as jnp
import numpy as np
from jax import lax
from jax.experimental import pallas as pl
from jax.experimental.pallas import tpu as pltpu
from jax.sharding import PartitionSpec as P

epsilon = 1e-06


def normalize(row_data, norm_gain, norm_bias):
    values = row_data.astype(jnp.float32)
    row_mean = jnp.mean(values, axis=-1, keepdims=True)
    centred = values - row_mean
    inv_std = lax.rsqrt(jnp.mean(centred * centred, axis=-1, keepdims=True) + epsilon)
    standard = centred * inv_std
    normed = (standard * norm_gain + norm_bias).astype(jnp.bfloat16)
    return (standard, inv_std, normed)


def contract_tokens(left_rows, right_rows):
    return lax.dot_general(
        left_rows, right_rows, (((0,), (0,)), ((), ())), preferred_element_type=jnp.float32
    )


def body(first_out, second_out, grad_first, grad_second, w_up, w_down, norm_gain, norm_bias):
    own_rows = first_out.shape[0]
    up_full, down_full = (
        lax.all_gather(w_up, "dp", axis=0, tiled=True),
        lax.all_gather(w_down, "dp", axis=1, tiled=True),
    )
    first_all, grad_all = (
        lax.all_gather(first_out, "tensor", axis=0, tiled=True),
        lax.all_gather(grad_second, "tensor", axis=0, tiled=True),
    )
    standard_all, inv_std_all, normed = normalize(first_all, norm_gain, norm_bias)
    offset = lax.axis_index("tensor") * own_rows
    standard = lax.dynamic_slice_in_dim(standard_all, offset, own_rows, 0)
    inv_std = lax.dynamic_slice_in_dim(inv_std_all, offset, own_rows, 0)
    preact = jnp.dot(normed, up_full, preferred_element_type=jnp.float32)
    hidden = jax.nn.gelu(preact).astype(jnp.bfloat16)
    branch = lax.psum_scatter(
        jnp.dot(hidden, down_full, preferred_element_type=jnp.float32).astype(jnp.bfloat16),
        "tensor",
        scatter_dimension=0,
        tiled=True,
    ).astype(jnp.float32)
    second_in = (second_out.astype(jnp.float32) - branch).astype(jnp.bfloat16)
    tokens = own_rows * lax.axis_size("tensor") * lax.axis_size("dp")
    grad_scale = tokens ** (-0.5)
    grad_down_part = contract_tokens(hidden, grad_all)
    grad_down = (
        lax.psum_scatter(
            grad_down_part.astype(jnp.bfloat16), "dp", scatter_dimension=1, tiled=True
        ).astype(jnp.float32)
        * grad_scale
    )
    grad_hidden = lax.dot_general(
        grad_all, down_full, (((1,), (1,)), ((), ())), preferred_element_type=jnp.float32
    )
    grad_pre = jax.vjp(jax.nn.gelu, preact)[1](grad_hidden)[0].astype(jnp.bfloat16)
    grad_up_part = contract_tokens(normed, grad_pre)
    grad_up = (
        lax.psum_scatter(
            grad_up_part.astype(jnp.bfloat16), "dp", scatter_dimension=0, tiled=True
        ).astype(jnp.float32)
        * grad_scale
    )
    grad_normed = lax.psum_scatter(
        lax.dot_general(
            grad_pre, up_full, (((1,), (1,)), ((), ())), preferred_element_type=jnp.float32
        ).astype(jnp.bfloat16),
        "tensor",
        scatter_dimension=0,
        tiled=True,
    ).astype(jnp.float32)
    grad_std = grad_normed * norm_gain
    grad_rows = inv_std * (
        grad_std
        - jnp.mean(grad_std, axis=-1, keepdims=True)
        - standard * jnp.mean(grad_std * standard, axis=-1, keepdims=True)
    )
    grad_first_in = grad_first.astype(jnp.float32) + grad_rows
    local_stats = jnp.stack([jnp.sum(grad_normed * standard, axis=0), jnp.sum(grad_normed, axis=0)])
    grad_norm = lax.psum(local_stats, ("tensor", "dp")) * grad_scale
    return (second_in, grad_first_in, grad_up, grad_down, grad_norm)


def span(index, size):
    return pl.ds(pl.multiple_of(index * size, size), size)


def flipped(index, mask, bits):
    for bit in range(bits):
        if mask >> bit & 1:
            step = 1 << bit
            index = index + (1 - 2 * ((index // step) % 2)) * step
    return index


def nearness(own, n_dp):
    return lambda z: (abs(z - own), z)


def earliness(own, n_dp):
    def key(z):
        edge = min(z, n_dp - 1 - z)
        return (z != own, edge, abs(z - own) if edge == 0 else -abs(z - own))

    return key


def ranked_place(dp, n_dp, rank, ranking=nearness):
    place = 0
    for own in range(n_dp):
        ranked = sorted(range(n_dp), key=ranking(own, n_dp))
        for k in range(n_dp):
            here = jnp.logical_and(dp == own, jnp.equal(rank, k))
            place = place + jnp.where(here, ranked[k], 0)
    return place


def remote(src, dst, sems, index, peer):
    return pltpu.make_async_remote_copy(
        src_ref=src,
        dst_ref=dst,
        send_sem=sems[0].at[index],
        recv_sem=sems[1].at[index],
        device_id=peer,
        device_id_type=pl.DeviceIdType.MESH,
    )


def standardize(row_data):
    values = row_data.astype(jnp.float32)
    centred = values - jnp.mean(values, axis=-1, keepdims=True)
    inv_std = lax.rsqrt(jnp.mean(centred * centred, axis=-1, keepdims=True) + epsilon)
    return centred * inv_std, inv_std


def fused_kernel(
    n_groups, n_tensor, n_dp, grad_scale,
    first_ref, second_ref, grad_first_in_ref, grad_ref, w_up_ref, w_down_ref, gain_ref, bias_ref,
    second_in_ref, grad_first_ref, grad_norm_ref, up_out, down_out,
    normed_all, grad_all, up_ref, down_ref, hidden_ref, slope_ref, pre_ref, g_up_ref, g_down_ref, own_normed,
    partials, fold, moving, stat_line, stat_fold, local_sem,
    row_send, row_recv, column_send, column_recv, weight_send, weight_recv, share_send, share_recv,
    fold_send, fold_recv, line_send, line_recv, grads_send, grads_recv,
    stat_send, stat_recv, pair_send, pair_recv,
):
    group, tensor, dp = (lax.axis_index(name) for name in ("groups", "tensor", "dp"))
    bits = n_tensor.bit_length() - 1
    rows, width = first_ref.shape
    column = rows * n_tensor
    depth = w_up_ref.shape[0]
    units = w_up_ref.shape[1] // n_dp
    part = depth // n_groups
    piece = units // n_groups
    tokens = (normed_all, grad_all)
    row_sems, column_sems = (row_send, row_recv), (column_send, column_recv)
    weight_sems, share_sems = (weight_send, weight_recv), (share_send, share_recv)
    fold_sems, line_sems = (fold_send, fold_recv), (line_send, line_recv)
    grads_sems, stat_sems, pair_sems = (
        (grads_send, grads_recv), (stat_send, stat_recv), (pair_send, pair_recv),
    )

    def cut_of(z, mask):
        return span(z * n_tensor + flipped(tensor, mask, bits), rows)

    def block(a, mask, z):
        return tokens[a].at[cut_of(z, mask), :]

    def tensor_peer(bit):
        return {"tensor": flipped(tensor, 1 << bit, bits)}

    def on_line(place):
        return jnp.logical_and(place >= 0, place <= n_dp - 1)

    def peer_at(place):
        return {"dp": (place + n_dp) % n_dp}

    def row_copy(a, side, z, own):
        src = grad_ref if a == 1 and own else block(a, 0, z)
        return remote(src, block(a, 0, z), row_sems, (a, side, z), peer_at(dp + 1 - 2 * side))

    def row_side(z):
        return jnp.where(z < dp, 0, 1)

    def column_copy(a, mask, z, bit, own=False):
        src = grad_ref if a == 1 and own else block(a, mask, z)
        return remote(src, block(a, mask, z), column_sems, (a, mask | 1 << bit, z), tensor_peer(bit))

    def column_arrival(a, mask, z):
        here = block(a, mask, z)
        bit = (mask & -mask).bit_length() - 1
        return remote(here, here, column_sems, (a, mask, z), tensor_peer(bit))

    def next_bits(mask):
        top = bits if mask == 0 else (mask & -mask).bit_length() - 1
        return list(reversed(range(top)))

    through = sorted((m for m in range(1, n_tensor) if next_bits(m)), reverse=True)
    final = [m for m in range(1, n_tensor) if not next_bits(m)]

    def send_own(a):
        for side in range(2):
            pl.when(on_line(dp + 1 - 2 * side))(lambda side=side: row_copy(a, side, dp, True).start())
        for bit in next_bits(0):
            column_copy(a, 0, dp, bit, True).start()

    def row_step(z):
        side = row_side(z)
        for a in (1, 0):
            row_copy(a, side, z, False).wait_recv()
            pl.when(on_line(dp + 1 - 2 * side))(lambda a=a: row_copy(a, side, z, False).start())
            for bit in next_bits(0):
                column_copy(a, 0, z, bit).start()

    def column_step(z):
        for mask in through:
            for a in (1, 0):
                column_arrival(a, mask, z).wait_recv()
                for bit in next_bits(mask):
                    column_copy(a, mask, z, bit).start()

    def settle_step(z):
        for mask in final:
            for a in (1, 0):
                column_arrival(a, mask, z).wait_recv()

    def weight_view(kind, source, owner):
        if kind == 0:
            return up_ref.at[span(source * n_groups + owner, part), :]
        return down_ref.at[span(owner, piece), span(source, depth)]

    def weight_copy(kind, target):
        if kind == 0:
            src = w_up_ref.at[span(group, part), span(target, units)]
        else:
            src = w_down_ref.at[span(target * n_groups + group, piece), :]
        s = (target + n_dp - dp) % n_dp
        return remote(src, weight_view(kind, dp, group), weight_sems, (kind, s), {"dp": target})

    def weight_arrival(kind, source):
        here = weight_view(kind, source, group)
        s = (dp + n_dp - source) % n_dp
        return remote(here, here, weight_sems, (kind, s), {"dp": (dp + s) % n_dp})

    def share_copy(kind, source, h):
        here = weight_view(kind, source, group)
        return remote(here, here, share_sems, (kind, source, h), {"groups": (group + h) % n_groups})

    def share_arrival(kind, source, h):
        here = weight_view(kind, source, (group + n_groups - h) % n_groups)
        return remote(here, here, share_sems, (kind, source, h), {"groups": (group + h) % n_groups})

    def weight_step(kind, source):
        weight_arrival(kind, source).wait_recv()
        for h in range(1, n_groups):
            share_copy(kind, source, h).start()

    def share_step(kind):
        for k in range(1, n_dp):
            for h in range(1, n_groups):
                share_arrival(kind, near[k], h).wait_recv()

    half = column // 2

    @jax.named_scope("useup")
    def use_up(z):
        @pl.loop(0, column // half)
        def _(i):
            cut = span(z * (column // half) + i, half)
            preact = jnp.dot(normed_all[cut, :], up_ref[...], preferred_element_type=jnp.float32)
            root = (2.0 / np.pi) ** 0.5
            square = preact * preact
            bend = jnp.tanh(root * (preact + 0.044715 * (square * preact)))
            gate = 0.5 * (1.0 + bend)
            hidden_ref[cut, :] = (preact * gate).astype(hidden_ref.dtype)
            slope_ref[cut, :] = gate + (0.5 * preact) * (1.0 - bend * bend) * (
                root * (1.0 + 3.0 * 0.044715 * square)
            )

    @jax.named_scope("usedown")
    def use_down(z):
        @pl.loop(0, column // half)
        def _(i):
            cut = span(z * (column // half) + i, half)
            grad_hidden = lax.dot_general(
                grad_all[cut, :], down_ref[...], (((1,), (1,)), ((), ())),
                preferred_element_type=jnp.float32,
            )
            pre_ref[cut, :] = (grad_hidden * slope_ref[cut, :]).astype(pre_ref.dtype)

    @jax.named_scope("wblk")
    def weight_block(kind, z):
        cut = span(z, depth)
        if kind == 0:
            g_up_ref[z] = contract_tokens(normed_all[:, cut], pre_ref[...]).astype(g_up_ref.dtype)
        else:
            g_down_ref[z] = contract_tokens(hidden_ref[...], grad_all[:, cut]).astype(
                g_down_ref.dtype
            )

    def grads_view(kind, source):
        if kind == 0:
            return up_out.at[:, span(source, units)]
        return down_out.at[span(source, units), :]

    def grads_copy(kind, z):
        src = (g_up_ref, g_down_ref)[kind].at[z]
        s = (z + n_dp - dp) % n_dp
        return remote(src, grads_view(kind, dp), grads_sems, (kind, s), peer_at(z))

    def grads_arrival(kind, s):
        here = grads_view(kind, (dp + n_dp - s) % n_dp)
        return remote(here, here, grads_sems, (kind, s), {"dp": (dp + s) % n_dp})

    slots = {}
    for bit in range(bits):
        for mask in range(0, n_tensor, 2 << bit):
            slots[bit, mask] = len(slots)
    last = slots[bits - 1, 0]

    def current(a, bit, mask, z):
        if bit == 0:
            return partials.at[a, cut_of(z, mask), :]
        return fold.at[a, slots[bit - 1, mask], z]

    def fold_copy(a, bit, mask, z):
        slot = slots[bit, mask ^ 1 << bit]
        return remote(
            current(a, bit, mask, z), fold.at[a, slot, z], fold_sems, (a, slot, z), tensor_peer(bit)
        )

    def fold_arrival(a, bit, mask, z):
        slot = slots[bit, mask]
        here = fold.at[a, slot, z]
        return remote(here, here, fold_sems, (a, slot, z), tensor_peer(bit))

    def add_into(ref, other):
        @pl.loop(0, rows // 16)
        def _(i):
            cut = pl.ds(pl.multiple_of(i * 16, 16), 16)
            ref[cut, :] = (
                ref[cut, :].astype(jnp.float32) + other[cut, :].astype(jnp.float32)
            ).astype(ref.dtype)

    def sent_masks(bit):
        masks = [m for m in range(n_tensor) if m % (1 << bit) == 0 and m >> bit & 1]
        return sorted(masks, reverse=True)

    def kept_masks(bit):
        return sorted(range(0, n_tensor, 2 << bit), reverse=True)

    @jax.named_scope("mul")
    def multiply(z):
        @pl.loop(0, column // half)
        def _(i):
            cut = span(z * (column // half) + i, half)
            partials[0, cut, :] = jnp.dot(
                hidden_ref[cut, :], down_ref[...], preferred_element_type=jnp.float32
            ).astype(partials.dtype)
            partials[1, cut, :] = lax.dot_general(
                pre_ref[cut, :], up_ref[...], (((1,), (1,)), ((), ())),
                preferred_element_type=jnp.float32,
            ).astype(partials.dtype)

        for mask in sent_masks(0):
            for a in range(2):
                fold_copy(a, 0, mask, z).start()

    def folded(a, bit, mask, z):
        fold_arrival(a, bit, mask, z).wait_recv()
        add_into(fold.at[a, slots[bit, mask], z], current(a, bit, mask, z))
        if bit + 1 < bits and mask in sent_masks(bit + 1):
            fold_copy(a, bit + 1, mask, z).start()

    @jax.named_scope("inner")
    def inner_folds(z):
        for bit in range(bits - 1):
            for mask in kept_masks(bit):
                for a in range(2):
                    folded(a, bit, mask, z)

    def line_side(z):
        return jnp.where(z > dp, 0, 1)

    def line_copy(a, side, z, relayed):
        here = moving.at[side, a, z]
        src = here if relayed else fold.at[a, last, z]
        return remote(src, here, line_sems, (side, a, z), peer_at(dp + 1 - 2 * side))

    def line_arrival(a, side, z):
        here = moving.at[side, a, z]
        return remote(here, here, line_sems, (side, a, z), peer_at(dp + 1 - 2 * side))

    @jax.named_scope("fwd")
    def forward(z):
        side = line_side(z)
        behind = on_line(dp - 1 + 2 * side)
        for a in range(2):
            folded(a, bits - 1, 0, z)

            @pl.when(behind)
            def _(a=a):
                line_arrival(a, side, z).wait_recv()
                add_into(moving.at[side, a, z], fold.at[a, last, z])
                line_copy(a, side, z, True).start()

            @pl.when(jnp.logical_not(behind))
            def _(a=a):
                line_copy(a, side, z, False).start()

    near = [ranked_place(dp, n_dp, k) for k in range(n_dp)]
    far = list(reversed(near))
    early = [ranked_place(dp, n_dp, k, earliness) for k in range(n_dp)]
    inside = jnp.logical_and(on_line(dp - 1), on_line(dp + 1))

    barrier = pltpu.get_barrier_semaphore()
    peers = [{"dp": (dp + s) % n_dp} for s in range(1, n_dp)]
    peers += [tensor_peer(bit) for bit in range(bits)]
    peers += [{"groups": (group + s) % n_groups} for s in range(1, n_groups)]
    for peer in peers:
        pl.semaphore_signal(barrier, inc=1, device_id=peer, device_id_type=pl.DeviceIdType.MESH)

    local = [
        pltpu.make_async_copy(grad_ref, block(1, 0, dp), local_sem.at[1]),
        pltpu.make_async_copy(
            w_up_ref.at[:, span(dp, units)], up_ref.at[span(dp, depth), :], local_sem.at[2]
        ),
        pltpu.make_async_copy(
            w_down_ref.at[span(dp, units), :], down_ref.at[:, span(dp, depth)], local_sem.at[3]
        ),
    ]
    for copy in local:
        copy.start()

    @pl.loop(0, rows // 16)
    def _(i):
        cut = pl.ds(pl.multiple_of(i * 16, 16), 16)
        standard, _ = standardize(first_ref[cut, :])
        own_normed[cut, :] = (standard * gain_ref[...] + bias_ref[...]).astype(own_normed.dtype)

    settle = pltpu.make_async_copy(own_normed, block(0, 0, dp), local_sem.at[0])
    settle.start()
    settle.wait()
    with jax.named_scope("greet"):
        pl.semaphore_wait(barrier, len(peers))
    send_own(1)
    send_own(0)

    def weight_start(kinds, conditions):
        for kind in kinds:
            for k in range(1, n_dp):
                @pl.when(conditions(jnp.abs(near[k] - dp), inner(near[k])))
                def _(kind=kind, k=k):
                    weight_copy(kind, near[k]).start()

    def inner(z):
        return jnp.logical_and(z >= 1, z <= n_dp - 2)

    both = jnp.logical_and
    outside = jnp.logical_not(inside)
    with jax.named_scope("rows1"):
        row_step(near[1])
    weight_start((0, 1), lambda gap, to_inner: both(outside, gap == 1))
    with jax.named_scope("rows2"):
        for k in range(2, min(3, n_dp)):
            row_step(near[k])
    weight_start((0, 1), lambda gap, to_inner: both(inside, to_inner))
    weight_start((0,), lambda gap, to_inner: both(outside, gap > 1))
    with jax.named_scope("rows3"):
        for k in range(3, n_dp):
            row_step(near[k])
    weight_start((0, 1), lambda gap, to_inner: both(inside, jnp.logical_not(to_inner)))
    weight_start((1,), lambda gap, to_inner: both(outside, gap > 1))

    with jax.named_scope("cols1"):
        for k in range(n_dp - 1):
            column_step(near[k])
            if k >= 1:
                weight_step(0, early[k])
    with jax.named_scope("weights0"):
        for copy in local:
            copy.wait()
        weight_step(0, early[n_dp - 1])
        share_step(0)
    for k in range(n_dp - 1):
        with jax.named_scope("settle"):
            settle_step(near[k])
        use_up(near[k])
        if k >= 1:
            with jax.named_scope("weights1"):
                weight_step(1, early[k])
    with jax.named_scope("cols2"):
        column_step(near[n_dp - 1])
    with jax.named_scope("settle"):
        settle_step(near[n_dp - 1])
    use_up(near[n_dp - 1])

    def grads_step(kind, z):
        weight_block(kind, z)
        grads_copy(kind, z).start()

    grads_step(1, far[0])
    with jax.named_scope("weights1"):
        weight_step(1, early[n_dp - 1])
    for k in range(1, n_dp - 1):
        grads_step(1, far[k])
    with jax.named_scope("weights1"):
        share_step(1)

    for k in range(n_dp):
        use_down(far[k])
        multiply(far[k])
        if k >= 1:
            inner_folds(far[k - 1])
    inner_folds(dp)

    @pl.loop(0, n_dp)
    def _(k):
        weight_block(0, ranked_place(dp, n_dp, n_dp - 1 - k))

    def late_grads(k):
        grads_copy(0, far[k]).start()

    pl.when(inside)(lambda: late_grads(0))
    weight_block(1, dp)
    own_grads = [
        pltpu.make_async_copy(g_up_ref.at[dp], up_out.at[:, span(dp, units)], local_sem.at[0]),
        pltpu.make_async_copy(g_down_ref.at[dp], down_out.at[span(dp, units), :], local_sem.at[1]),
    ]
    for copy in own_grads:
        copy.start()
    for k in range(n_dp - 1):
        forward(far[k])
    pl.when(jnp.logical_not(inside))(lambda: late_grads(0))
    for k in range(1, n_dp - 2):
        late_grads(k)

    with jax.named_scope("last"):
        for a in range(2):
            folded(a, bits - 1, 0, dp)
            for side in range(2):
                behind = on_line(dp - 1 + 2 * side)

                @pl.when(behind)
                def _(a=a, side=side):
                    line_arrival(a, side, dp).wait_recv()

                @pl.when(jnp.logical_not(behind))
                def _(a=a, side=side):
                    moving[side, a, dp] = jnp.zeros((rows, width), moving.dtype)

    stat_line[dp] = jnp.zeros(stat_line.shape[1:], jnp.float32)

    @pl.loop(0, rows // 16)
    def _(i):
        cut = pl.ds(pl.multiple_of(i * 16, 16), 16)

        def total(a):
            return (
                fold[a, last, dp, cut, :].astype(jnp.float32)
                + moving[0, a, dp, cut, :].astype(jnp.float32)
                + moving[1, a, dp, cut, :].astype(jnp.float32)
            )

        second_in_ref[cut, :] = (second_ref[cut, :].astype(jnp.float32) - total(0)).astype(
            second_in_ref.dtype
        )
        standard, inv_std = standardize(first_ref[cut, :])
        grad_normed = total(1)
        stat_line[dp, 0:1, :] += jnp.sum(grad_normed * standard, axis=0, keepdims=True)
        stat_line[dp, 1:2, :] += jnp.sum(grad_normed, axis=0, keepdims=True)
        grad_std = grad_normed * gain_ref[...]
        grad_rows = inv_std * (
            grad_std
            - jnp.mean(grad_std, axis=-1, keepdims=True)
            - standard * jnp.mean(grad_std * standard, axis=-1, keepdims=True)
        )
        grad_first_ref[cut, :] = grad_first_in_ref[cut, :].astype(jnp.float32) + grad_rows

    def stat_copy(s):
        here = stat_line.at[dp]
        return remote(here, here, stat_sems, s, {"dp": (dp + s) % n_dp})

    def stat_arrival(s):
        here = stat_line.at[(dp + n_dp - s) % n_dp]
        return remote(here, here, stat_sems, s, {"dp": (dp + s) % n_dp})

    with jax.named_scope("stats"):
        for s in range(1, n_dp):
            stat_copy(s).start()
        for k in range(max(1, n_dp - 2), n_dp - 1):
            late_grads(k)
        for s in range(1, n_dp):
            stat_arrival(s).wait_recv()
        sums = stat_line[0]
        for source in range(1, n_dp):
            sums = sums + stat_line[source]
        for bit in range(bits):
            stat_fold[bit, 0] = sums
            copy = remote(
                stat_fold.at[bit, 0], stat_fold.at[bit, 1], pair_sems, bit, tensor_peer(bit)
            )
            copy.start()
            copy.wait()
            sums = stat_fold[bit, 0] + stat_fold[bit, 1]
        grad_norm_ref[...] = sums[0:2] * grad_scale

    with jax.named_scope("drain"):
        for s in range(1, n_dp):
            stat_copy(s).wait_send()
            for kind in range(2):
                grads_arrival(kind, s).wait_recv()
                grads_copy(kind, (dp + s) % n_dp).wait_send()
                weight_copy(kind, (dp + s) % n_dp).wait_send()
                for h in range(1, n_groups):
                    share_copy(kind, (dp + s) % n_dp, h).wait_send()
        for copy in own_grads:
            copy.wait()
        for a in range(2):
            for side in range(2):
                pl.when(on_line(dp + 1 - 2 * side))(
                    lambda a=a, side=side: row_copy(a, side, dp, True).wait_send()
                )
            for k in range(1, n_dp):
                side = row_side(near[k])
                pl.when(on_line(dp + 1 - 2 * side))(
                    lambda a=a, side=side, k=k: row_copy(a, side, near[k], False).wait_send()
                )
            for z in range(n_dp):
                for mask in [0] + through:
                    for bit in next_bits(mask):
                        column_copy(a, mask, z, bit).wait_send()
                for bit in range(bits):
                    for mask in sent_masks(bit):
                        fold_copy(a, bit, mask, z).wait_send()
            for k in range(n_dp - 1):
                line_copy(a, line_side(far[k]), far[k], True).wait_send()


ANY = pl.BlockSpec(memory_space=pl.ANY)
VMEM = pl.BlockSpec(memory_space=pltpu.VMEM)
DMA = pltpu.SemaphoreType.DMA


def spread_body(sizes, first_out, second_out, grad_first, grad_second, w_up, w_down, norm_gain, norm_bias):
    n_groups, n_tensor, n_dp = sizes
    rows, width = first_out.shape
    tokens = rows * n_tensor * n_dp
    units = w_up.shape[1] // n_dp
    bits = n_tensor.bit_length() - 1
    half = jnp.bfloat16
    grad_scale = tokens ** (-0.5)
    gain, bias = norm_gain.reshape(1, -1), norm_bias.reshape(1, -1)
    depth = w_up.shape[0]
    second_in, grad_first_in, grad_norm, up_out, down_out = pl.pallas_call(
        functools.partial(fused_kernel, n_groups, n_tensor, n_dp, grad_scale),
        out_shape=(
            jax.ShapeDtypeStruct((rows, width), half),
            jax.ShapeDtypeStruct((rows, width), jnp.float32),
            jax.ShapeDtypeStruct((2, width), jnp.float32),
            jax.ShapeDtypeStruct(w_up.shape, half),
            jax.ShapeDtypeStruct(w_down.shape, half),
        ),
        in_specs=[VMEM] * 3 + [ANY] * 3 + [VMEM] * 2,
        out_specs=(VMEM,) * 3 + (ANY,) * 2,
        scratch_shapes=[
            pltpu.VMEM((tokens, width), half),
            pltpu.VMEM((tokens, width), half),
            pltpu.VMEM((width, units), half),
            pltpu.VMEM((units, width), half),
            pltpu.VMEM((tokens, units), half),
            pltpu.VMEM((tokens, units), jnp.float32),
            pltpu.VMEM((tokens, units), half),
            pltpu.VMEM((n_dp, depth, units), half),
            pltpu.VMEM((n_dp, units, depth), half),
            pltpu.VMEM((rows, width), half),
            pltpu.VMEM((2, tokens, width), half),
            pltpu.VMEM((2, n_tensor - 1, n_dp, rows, width), half),
            pltpu.VMEM((2, 2, n_dp, rows, width), half),
            pltpu.VMEM((n_dp, 8, width), jnp.float32),
            pltpu.VMEM((bits, 2, 8, width), jnp.float32),
            DMA((4,)),
        ]
        + [DMA((2, 2, n_dp))] * 2
        + [DMA((2, n_tensor, n_dp))] * 2
        + [DMA((2, n_dp))] * 2
        + [DMA((2, n_dp, n_groups))] * 2
        + [DMA((2, n_tensor - 1, n_dp))] * 2
        + [DMA((2, 2, n_dp))] * 2
        + [DMA((2, n_dp))] * 2
        + [DMA((n_dp,))] * 2
        + [DMA((bits,))] * 2,
        compiler_params=pltpu.CompilerParams(
            collective_id=0, has_side_effects=True, vmem_limit_bytes=60 << 20
        ),
        name="spread_backward",
    )(first_out, second_out, grad_first, grad_second, w_up, w_down, gain, bias)
    grad_up = up_out.astype(jnp.float32) * grad_scale
    grad_down = down_out.astype(jnp.float32) * grad_scale
    return second_in, grad_first_in, grad_up, grad_down, grad_norm


def choose(sizes, *args):
    first_out, w_up = args[0], args[4]
    n_groups, n_tensor, n_dp = sizes
    tokens = first_out.shape[0] * n_tensor * n_dp
    fits = (
        n_tensor > 1
        and n_dp > 1
        and n_dp % 2 == 0
        and n_tensor & (n_tensor - 1) == 0
        and w_up.shape[1] % (n_dp * n_groups * 128) == 0
        and w_up.shape[0] % (n_groups * 128) == 0
    )
    if fits and tokens <= w_up.shape[1]:
        return spread_body(sizes, *args)
    return body(*args)


def solution(mesh):
    in_specs = (
        P(("groups", "tensor", "dp"), None),
        P(("groups", "tensor", "dp"), None),
        P(("groups", "tensor", "dp"), None),
        P(("groups", "tensor", "dp"), None),
        P("dp", "tensor"),
        P("tensor", "dp"),
        P(),
        P(),
    )
    out_specs = (
        P(("groups", "tensor", "dp"), None),
        P(("groups", "tensor", "dp"), None),
        P(("groups", "dp"), "tensor"),
        P(("groups", "tensor"), "dp"),
        P("groups", None),
    )
    sizes = tuple(mesh.shape[name] for name in ("groups", "tensor", "dp"))
    return jax.shard_map(functools.partial(choose, sizes), mesh=mesh, in_specs=in_specs, out_specs=out_specs, check_vma=False)
```

time: 164 us -> 157 us (0.957)
  Pallas kernels: 157 us -> 148 us
    pallas_call x1, Pallas kernels: 157 us -> 148 us  [spread_body(): pl.pallas_call(functools.partial(fused_kernel, n_groups, n_tensor, n_dp,...]
where the time goes in v1:
time: 157 us; the launch traced here: 155 us
  Pallas kernels  148 us (94%)
  other arithmetic  4.39 us (3%)
  local copies, waits for them, and re-layouts  2.11 us (1%)
    pallas_call x1, Pallas kernels, spread_body(): pl.pallas_call(functools.partial(fused_kernel, n_groups, n_tensor, n_dp,...  148 us

profile of v1, /device:TPU:0, one launch (start us, length us, event | category | flops | bytes accessed | tf_op | source)
XLA Modules:
  0.0 155.3 jit_solution(17105333788905527804)
XLA Ops:
  0.6 148.2 %spread_backward.1 = (bf16[128,1024]{1,0:T(8,128)(2,1)}, f32[128,1024]{1,0:T(8,128)}, f32[2,1024]{1,0:T(2,128)}, bf16[256,2048]{1,0:T(8,128)(2,1)}, bf16[2048,256]{1,0:T(8,128)(2,1)}) custom-call(bf16[128,1024]{1,0:T(8,128)(2,1)} %first_ref.1, bf16[128,1024]{1,0:T(8,128)(2,1)} %second_ref.1, bf16[128,1024]{1,0:T(8,128)(2,1)} %grad_first_in_ref.1, ...), custom_call_target="tpu_custom_call" | custom-call | tf_op jit(solution)/shard_map/spread_backward/pallas_call | solution.py:663
  148.8 0.0 copy-start
  148.8 2.9 %convert_multiply_fusion.1 = f32[256,2048]{1,0:T(8,128)} fusion(bf16[256,2048]{1,0:T(8,128)(2,1)} %get-tuple-element.12), kind=kLoop, calls=%fused_computation.1 | loop fusion | flops 1048576 | bytes 3145728 | tf_op jit(solution)/shard_map/mul | solution.py:706
  151.7 0.0 copy-done
  151.7 0.0 copy-start.2
  151.7 0.0 copy-start.1
  151.7 0.0 copy-start.3
  151.7 1.5 convert_multiply_fusion
  153.2 0.0 copy-done.2
  153.2 0.7 copy.16
  154.0 0.0 copy-done.1
  154.0 0.8 copy.17
  154.7 0.0 copy-done.3
  154.8 0.6 copy.18
Async XLA Ops:
  148.8 2.9 %copy-start = (bf16[2048,256]{1,0:T(8,128)(2,1)S(1)}, bf16[2048,256]{1,0:T(8,128)(2,1)}, u32[]{:S(2)}) copy-start(bf16[2048,256]{1,0:T(8,128)(2,1)} %get-tuple-element.13) | copy-start | bytes 3145732
  151.7 1.5 copy-start.2
  151.7 2.2 %copy-start.1 = (f32[128,1024]{1,0:T(8,128)S(1)}, f32[128,1024]{1,0:T(8,128)}, u32[]{:S(2)}) copy-start(f32[128,1024]{1,0:T(8,128)} %get-tuple-element.21) | copy-start | bytes 1572868
  151.7 3.0 %copy-start.3 = (f32[2,1024]{1,0:T(2,128)S(1)}, f32[2,1024]{1,0:T(2,128)}, u32[]{:S(2)}) copy-start(f32[2,1024]{1,0:T(2,128)} %get-tuple-element.24) | copy-start | bytes 24580

commit v2 on v1

--- a/solution.py
+++ b/solution.py
@@ -473,32 +473,52 @@
         for k in range(2, min(3, n_dp)):
             row_step(near[k])
     weight_start((0, 1), lambda gap, to_inner: both(inside, to_inner))
+    weight_start((0, 1), lambda gap, to_inner: both(inside, both(gap == 1, jnp.logical_not(to_inner))))
     weight_start((0,), lambda gap, to_inner: both(outside, gap > 1))
-    with jax.named_scope("rows3"):
-        for k in range(3, n_dp):
-            row_step(near[k])
-    weight_start((0, 1), lambda gap, to_inner: both(inside, jnp.logical_not(to_inner)))
+
+    def far_rows():
+        with jax.named_scope("rows3"):
+            for k in range(3, n_dp):
+                row_step(near[k])
+
+    pl.when(inside)(far_rows)
+    weight_start((), lambda gap, to_inner: both(inside, both(gap == 1, jnp.logical_not(to_inner))))
+    weight_start((0, 1), lambda gap, to_inner: both(inside, both(gap > 1, jnp.logical_not(to_inner))))
+    with jax.named_scope("cols1"):
+        column_step(near[0])
+        weight_step(0, early[1])
+        for k in range(1, n_dp - 1):
+            column_step(near[k])
+        for k in range(2, n_dp):
+            weight_step(0, early[k])
     weight_start((1,), lambda gap, to_inner: both(outside, gap > 1))
-
-    with jax.named_scope("cols1"):
-        for k in range(n_dp - 1):
-            column_step(near[k])
-            if k >= 1:
-                weight_step(0, early[k])
+    last_one = jnp.where(inside, early[n_dp - 2], early[1])
     with jax.named_scope("weights0"):
         for copy in local:
             copy.wait()
-        weight_step(0, early[n_dp - 1])
+        for k in range(1, n_dp):
+            pl.when(early[k] != last_one)(lambda k=k: weight_step(1, early[k]))
         share_step(0)
     for k in range(n_dp - 1):
         with jax.named_scope("settle"):
             settle_step(near[k])
         use_up(near[k])
-        if k >= 1:
-            with jax.named_scope("weights1"):
-                weight_step(1, early[k])
+    def own_partial():
+        with jax.named_scope("weights1"):
+            share_step(1)
+        use_down(dp)
+        multiply(dp)
+        inner_folds(dp)
+
+    @pl.when(outside)
+    def _():
+        weight_step(1, last_one)
+        far_rows()
+        own_partial()
+
     with jax.named_scope("cols2"):
         column_step(near[n_dp - 1])
+    pl.when(inside)(lambda: weight_step(1, last_one))
     with jax.named_scope("settle"):
         settle_step(near[n_dp - 1])
     use_up(near[n_dp - 1])
@@ -507,20 +527,15 @@
         weight_block(kind, z)
         grads_copy(kind, z).start()
 
-    grads_step(1, far[0])
-    with jax.named_scope("weights1"):
-        weight_step(1, early[n_dp - 1])
-    for k in range(1, n_dp - 1):
+    for k in range(n_dp - 1):
         grads_step(1, far[k])
-    with jax.named_scope("weights1"):
-        share_step(1)
-
-    for k in range(n_dp):
+    pl.when(inside)(own_partial)
+    for k in range(n_dp - 1):
         use_down(far[k])
         multiply(far[k])
         if k >= 1:
             inner_folds(far[k - 1])
-    inner_folds(dp)
+    inner_folds(far[n_dp - 2])
 
     @pl.loop(0, n_dp)
     def _(k):

time: 157 us -> 155 us (0.987); the launches traced: 155 us -> 155 us
  no operation moved by 1% of the time
where the time goes in v2:
time: 155 us
  Pallas kernels  148 us (95%)
  other arithmetic  4.39 us (3%)
  local copies, waits for them, and re-layouts  2.11 us (1%)
    pallas_call x1, Pallas kernels, spread_body(): pl.pallas_call(functools.partial(fused_kernel, n_groups, n_tensor, n_dp,...  148 us

profile of v2, /device:TPU:0, one launch (start us, length us, event | category | flops | bytes accessed | tf_op | source)
XLA Modules:
  0.0 155.1 jit_solution(1400681263680780811)
XLA Ops:
  0.6 147.9 %spread_backward.1 = (bf16[128,1024]{1,0:T(8,128)(2,1)}, f32[128,1024]{1,0:T(8,128)}, f32[2,1024]{1,0:T(2,128)}, bf16[256,2048]{1,0:T(8,128)(2,1)}, bf16[2048,256]{1,0:T(8,128)(2,1)}) custom-call(bf16[128,1024]{1,0:T(8,128)(2,1)} %first_ref.1, bf16[128,1024]{1,0:T(8,128)(2,1)} %second_ref.1, bf16[128,1024]{1,0:T(8,128)(2,1)} %grad_first_in_ref.1, ...), custom_call_target="tpu_custom_call" | custom-call | tf_op jit(solution)/shard_map/spread_backward/pallas_call | solution.py:678
  148.6 0.0 copy-start
  148.6 2.9 %convert_multiply_fusion.1 = f32[256,2048]{1,0:T(8,128)} fusion(bf16[256,2048]{1,0:T(8,128)(2,1)} %get-tuple-element.12), kind=kLoop, calls=%fused_computation.1 | loop fusion | flops 1048576 | bytes 3145728 | tf_op jit(solution)/shard_map/mul | solution.py:721
  151.5 0.0 copy-done
  151.5 0.0 copy-start.2
  151.5 0.0 copy-start.1
  151.5 0.0 copy-start.3
  151.5 1.5 convert_multiply_fusion
  153.0 0.0 copy-done.2
  153.0 0.7 copy.16
  153.7 0.0 copy-done.1
  153.7 0.8 copy.17
  154.5 0.0 copy-done.3
  154.5 0.6 copy.18
Async XLA Ops:
  148.6 2.9 %copy-start = (bf16[2048,256]{1,0:T(8,128)(2,1)S(1)}, bf16[2048,256]{1,0:T(8,128)(2,1)}, u32[]{:S(2)}) copy-start(bf16[2048,256]{1,0:T(8,128)(2,1)} %get-tuple-element.13) | copy-start | bytes 3145732
  151.5 1.5 copy-start.2
  151.5 2.2 %copy-start.1 = (f32[128,1024]{1,0:T(8,128)S(1)}, f32[128,1024]{1,0:T(8,128)}, u32[]{:S(2)}) copy-start(f32[128,1024]{1,0:T(8,128)} %get-tuple-element.21) | copy-start | bytes 1572868
  151.5 3.0 %copy-start.3 = (f32[2,1024]{1,0:T(2,128)S(1)}, f32[2,1024]{1,0:T(2,128)}, u32[]{:S(2)}) copy-start(f32[2,1024]{1,0:T(2,128)} %get-tuple-element.24) | copy-start | bytes 24580
